TPU v7x, 32 devices: a whole 2x2x4 slice. The times are simulated.
32 devices in a mesh: bpm: 4 (over y, x), cor: 8 (over z, core).
Axes of the slice: x: 2, y: 2, z: 4, core: 2. Of those that a mesh axis runs over, the one named last changes fastest.
Arguments:
- quad_bpm: bfloat16 [6144, 2048], P('cor', 'bpm'), may hold values from -0.078125 to 0.078125
- cor_quad: bfloat16 [6144, 6144], P('cor', 'bpm'), may hold values from -0.875 to 0.875
- step: float32 [6144], P(('bpm', 'cor')), may hold values from -6 to 6
- quad_order: int32 [6144], replicated, may hold values from 0 to 6143, each once
- bpm_mask: int32 [2048], P('bpm'), may hold values 0 or 1
- bpm_noise: float32 [2048], P('bpm'), may hold values from 0.5 to 2
Outputs:
- product: float32 [6144], P(('bpm', 'cor'))
Inputs may be any that keep to these rules, and one draw needn't show every extreme that they name: `quad_order`: each parameter drives exactly one quadrupole.
All inputs are finite; a program needn't handle non-finite values. No bound on the sum of `bpm_mask` on one device may be relied on, other than what follows from the above.
Results may differ from a plain program's by a relative error of at most 0.00035.
Values may be sent and summed in bfloat16 or wider, within the bound.
No kernel may reach another device: no remote copies, remote signals or barrier semaphores. Data moves between devices by JAX's collectives and lax.ppermute only.
A program may use at most 64 MiB of HBM per device.

v0:
```python
import jax
import jax.numpy as jnp
from jax import lax
from jax.sharding import PartitionSpec as P


def on_device(quad_bpm, cor_quad, step, quad_order, bpm_mask, bpm_noise):
    whole_step = lax.all_gather(step, ("bpm", "cor"), axis=0, tiled=True)
    u_vec = whole_step[quad_order]
    sens_full = lax.all_gather(cor_quad, "bpm", axis=1, tiled=True)
    scaled = (u_vec[None, :] * sens_full.astype(jnp.float32)).astype(jnp.bfloat16)
    weight = bpm_mask.astype(jnp.float32) / (bpm_noise * bpm_noise)
    rows_full = lax.all_gather(quad_bpm, "cor", axis=0, tiled=True)
    response = jnp.dot(scaled, rows_full, preferred_element_type=jnp.float32)
    weighted = (weight[None, :] * response).astype(jnp.bfloat16)
    back = lax.dot_general(
        sens_full, weighted, (((0,), (0,)), ((), ())), preferred_element_type=jnp.float32
    )
    d_vec = jnp.sum(rows_full.astype(jnp.float32) * back, axis=1)
    partial_value = jnp.zeros((quad_order.shape[0],), jnp.float32).at[quad_order].set(d_vec)
    total = lax.psum(partial_value, ("bpm", "cor"))
    share = step.shape[0]
    return lax.dynamic_slice_in_dim(total, lax.axis_index(("bpm", "cor")) * share, share, 0)


def solution(mesh):
    placed = (P("cor", "bpm"), P("cor", "bpm"), P(("bpm", "cor")), P(), P("bpm"), P("bpm"))
    return jax.shard_map(
        on_device, mesh=mesh, in_specs=placed, out_specs=P(("bpm", "cor")), check_vma=False
    )
```

profile of v0, /device:TPU:0, one launch (start us, length us, event | category | flops | bytes accessed | tf_op | source)
XLA Modules:
  0.0 260.7 jit_solution(18259405172421799365)
XLA Ops:
  6.5 0.0 all-gather.3.cloned.1.call-start
  6.5 2.3 copy.8
  8.8 0.0 all-gather.3.cloned.1.call-update
  8.9 0.0 all-gather.5.cloned.1.call-start
  8.9 0.7 all-gather.5.cloned.1.call-update
  9.6 0.9 dynamic-update-slice
  10.5 46.3 %all-reduce = f32[6144]{0:T(1024)S(1)} all-reduce(f32[6144]{0:T(1024)S(1)} %dynamic-update-slice), channel_id=1, replica_groups=mesh['bpm'=4,'cor'=8] {'bpm','cor'}, use_global_device_ids=true, to_apply=%add | all-reduce | flops 6144 | bytes 49152
  56.8 0.7 broadcast_clamp_fusion
  57.6 0.0 copy-start
  57.6 0.0 copy-start.1
  57.6 34.3 %gather_fusion = f32[6144]{0:T(1024)S(1)} fusion(f32[6144]{0:T(1024)S(1)} %all-reduce, s32[6144]{0:T(1024)S(1)} %get-tuple-element.5), kind=kCustom, calls=%fused_computation | custom fusion | bytes 73728 | tf_op jit(solution)/shard_map/gather | solution.py:9
  91.9 0.0 copy-done
  91.9 0.0 copy-done.1
  91.9 0.0 all-gather.3.cloned.1.call-done
  92.0 82.1 %all-gather.5.cloned.1.call-done = bf16[768,6144]{1,0:T(8,128)(2,1)} async-done(((bf16[768,1536]{1,0:T(8,128)(2,1)}), bf16[768,6144]{1,0:T(8,128)(2,1)}) %all-gather.5.cloned.1.call-update) | async-done | bytes 9437200 | tf_op jit(solution)/shard_map/all_gather | solution.py:10
  174.1 0.0 copy-start.2
  174.1 0.0 copy-start.3
  174.1 10.6 %multiply_convert_fusion.2 = bf16[768,512]{1,0:T(8,128)(2,1)S(1)} fusion(bf16[6144,512]{0,1:T(8,128)(2,1)} %all-gather.3.cloned.1.call-done, bf16[768,6144]{1,0:T(8,128)(2,1)} %all-gather.5.cloned.1.call-done, f32[6144]{0:T(1024)S(1)} %gather_fusion, f32[512]{0:T(512)S(1)} %multiply_divide_fusion), kind=kOutput, calls=%fused_computation.7 | convolution fusion | flops 4846780416 | bytes 16541696 | tf_op jit(solution)/shard_map/dot_general | solution.py:14
  184.7 0.0 copy-done.2
  184.7 0.0 copy-done.3
  184.8 5.9 %fusion = f32[6144]{0:T(1024)S(1)} fusion(bf16[6144,512]{0,1:T(8,128)(2,1)S(1)} %copy-done.3, bf16[768,512]{1,0:T(8,128)(2,1)S(1)} %multiply_convert_fusion.2, bf16[768,6144]{1,0:T(8,128)(2,1)S(1)} %copy-done.2), kind=kOutput, calls=%fused_computation.4 | convolution fusion | flops 4841269248 | bytes 16539648 | tf_op jit(solution)/shard_map/dot_general | solution.py:16
  190.7 23.0 %scatter_custom_fusion = f32[6144]{0:T(1024)S(1)} fusion(s32[6144]{0:T(1024)S(1)} %get-tuple-element.6, f32[6144]{0:T(1024)S(1)} %fusion, f32[]{:T(128)} %constant.7.clone.1), kind=kCustom, calls=%fused_computation.10 | custom fusion | bytes 24580 | tf_op jit(solution)/shard_map/scatter | solution.py:20
  213.7 39.5 %psum.7 = f32[6144]{0:T(1024)S(1)} all-reduce(f32[6144]{0:T(1024)S(1)} %scatter_custom_fusion), channel_id=1, replica_groups=mesh['bpm'=4,'cor'=8] {'bpm','cor'}, use_global_device_ids=true, to_apply=%region_2.0 | all-reduce | flops 6144 | bytes 49152 | tf_op jit(solution)/shard_map/psum | solution.py:21
  253.2 0.6 dynamic_slice.3
  (2 shorter events, 0.0 us)
Async XLA Ops:
  6.5 85.4 %all-gather.3.cloned.1.call-start = ((), (), s32[]{:S(2)}) async-start(), calls=%async_computation | async-start | bytes 7077888 | tf_op jit(solution)/shard_map/all_gather | solution.py:13
  8.9 165.2 %all-gather.5.cloned.1.call-start = ((), (), s32[]{:S(2)}) async-start(), calls=%async_computation.1 | async-start | bytes 11796480 | tf_op jit(solution)/shard_map/all_gather | solution.py:10
  57.6 34.3 %copy-start = (f32[512]{0:T(512)S(1)}, f32[512]{0:T(512)}, u32[]{:S(2)}) copy-start(f32[512]{0:T(512)} %param.11) | copy-start | bytes 6148
  57.6 34.3 %copy-start.1 = (s32[512]{0:T(512)S(1)}, s32[512]{0:T(512)}, u32[]{:S(2)}) copy-start(s32[512]{0:T(512)} %param.10) | copy-start | bytes 6148
  174.1 10.6 %copy-start.2 = (bf16[768,6144]{1,0:T(8,128)(2,1)S(1)}, bf16[768,6144]{1,0:T(8,128)(2,1)}, u32[]{:S(2)}) copy-start(bf16[768,6144]{1,0:T(8,128)(2,1)} %all-gather.5.cloned.1.call-done) | copy-start | bytes 28311556
  174.1 10.6 %copy-start.3 = (bf16[6144,512]{0,1:T(8,128)(2,1)S(1)}, bf16[6144,512]{0,1:T(8,128)(2,1)}, u32[]{:S(2)}) copy-start(bf16[6144,512]{0,1:T(8,128)(2,1)} %all-gather.3.cloned.1.call-done) | copy-start | bytes 18874372
Sparse Core Ops, SparseCore 0:
  9.0 68.3 all-gather.2
  79.2 94.8 all-gather.4
where the time goes:
time: 261 us
  blocking collectives  85.8 us (33%)
  waiting for transfers between devices  82.9 us (32%)
  local copies, waits for them, and re-layouts  61.2 us (23%)
  matrix products  16.5 us (6%)
  between operations  13.5 us (5%)
    all_gather x1, waiting for transfers between devices, on_device(): sens_full = lax.all_gather(cor_quad, 'bpm', axis=1, tiled=True)  82.1 us
    unnamed x1, blocking collectives  46.3 us
    psum x1, blocking collectives, on_device(): total = lax.psum(partial_value, ('bpm', 'cor'))  39.5 us
    gather x1, local copies, waits for them, and re-layouts, on_device(): u_vec = whole_step[quad_order]  34.3 us
    scatter x1, local copies, waits for them, and re-layouts, on_device(): jnp.zeros((quad_order.shape[0],), jnp.float32).at[quad_order].set(d_vec)  23 us
    dot_general x1, matrix products, on_device(): response = jnp.dot(scaled, rows_full, preferred_element_type=jnp.float32)  10.6 us
    dot_general x1, matrix products, on_device(): lax.dot_general(sens_full, weighted, (((0,), (0,)), ((), ())), preferred_...  5.92 us
  transfers between devices with their start and end apart: 2, of which 1 were waited for; matrix products, arithmetic and copies ran while one was open for 14% of the time, Pallas kernels for 0%

commit v1 on v0

--- a/solution.py
+++ b/solution.py
@@ -7,7 +7,9 @@
 def on_device(quad_bpm, cor_quad, step, quad_order, bpm_mask, bpm_noise):
     whole_step = lax.all_gather(step, ("bpm", "cor"), axis=0, tiled=True)
     u_vec = whole_step[quad_order]
-    sens_full = lax.all_gather(cor_quad, "bpm", axis=1, tiled=True)
+    sens_full = jnp.concatenate(
+        jax.lax.all_to_all(jnp.stack([cor_quad] * jax.lax.axis_size("bpm"), 0), "bpm", 0, 0), 1
+    )
     scaled = (u_vec[None, :] * sens_full.astype(jnp.float32)).astype(jnp.bfloat16)
     weight = bpm_mask.astype(jnp.float32) / (bpm_noise * bpm_noise)
     rows_full = lax.all_gather(quad_bpm, "cor", axis=0, tiled=True)

time: 261 us -> 297 us (1.14)
  blocking collectives: 85.8 us -> 179 us
  waiting for transfers between devices: 82.9 us -> 0.02 us
  local copies, waits for them, and re-layouts: 61.2 us -> 79.3 us
  starting transfers between devices: 0.04 us -> 6.07 us
    unnamed x1, blocking collectives: 46.3 us -> 139 us
    all_gather x1 -> x0, waiting for transfers between devices: 82.1 us -> none  [on_device(): sens_full = lax.all_gather(cor_quad, 'bpm', axis=1, tiled=True)]
    all_to_all x0 -> x1, local copies, waits for them, and re-layouts: none -> 12.7 us  [on_device(): jax.lax.all_to_all(jnp.stack([cor_quad] * jax.lax.axis_size('bpm'), 0), '...]
    all_to_all x0 -> x1, starting transfers between devices: none -> 6.07 us  [on_device(): jax.lax.all_to_all(jnp.stack([cor_quad] * jax.lax.axis_size('bpm'), 0), '...]
    another operation x0 -> x1, local copies, waits for them, and re-layouts: none -> 6.05 us  [on_device(): jnp.stack([cor_quad] * jax.lax.axis_size('bpm'), 0)]
  transfers between devices with their start and end apart: 2 -> 2, of which waited for: 1 -> 0; matrix products, arithmetic and copies ran while one was open for 14% -> 18% of each run, Pallas kernels for 0% -> 0%
where the time goes in v1:
time: 297 us; the launch traced here: 296 us
  blocking collectives  179 us (60%)
  local copies, waits for them, and re-layouts  79.3 us (27%)
  matrix products  18.8 us (6%)
  between operations  13.5 us (5%)
  starting transfers between devices  6.07 us (2%)
    unnamed x1, blocking collectives  139 us
    psum x1, blocking collectives, on_device(): total = lax.psum(partial_value, ('bpm', 'cor'))  39.2 us
    gather x1, local copies, waits for them, and re-layouts, on_device(): u_vec = whole_step[quad_order]  34.3 us
    scatter x1, local copies, waits for them, and re-layouts, on_device(): jnp.zeros((quad_order.shape[0],), jnp.float32).at[quad_order].set(d_vec)  23 us
    all_to_all x1, local copies, waits for them, and re-layouts, on_device(): jax.lax.all_to_all(jnp.stack([cor_quad] * jax.lax.axis_size('bpm'), 0), '...  12.7 us
    dot_general x1, matrix products, on_device(): response = jnp.dot(scaled, rows_full, preferred_element_type=jnp.float32)  11.6 us
    dot_general x1, matrix products, on_device(): lax.dot_general(sens_full, weighted, (((0,), (0,)), ((), ())), preferred_...  7.23 us
    all_to_all x1, starting transfers between devices, on_device(): jax.lax.all_to_all(jnp.stack([cor_quad] * jax.lax.axis_size('bpm'), 0), '...  6.07 us
  transfers between devices with their start and end apart: 2, of which 0 were waited for; matrix products, arithmetic and copies ran while one was open for 18% of the time, Pallas kernels for 0%

profile of v1, /device:TPU:0, one launch (start us, length us, event | category | flops | bytes accessed | tf_op | source)
XLA Modules:
  0.0 296.4 jit_solution(5007670301437909283)
XLA Ops:
  6.5 0.0 all-gather.2.cloned.1.call-start
  6.5 2.3 copy.10
  8.9 0.0 all-gather.2.cloned.1.call-update
  8.9 6.0 %stack.2 = bf16[4,768,1536]{2,1,0:T(8,128)(2,1)} broadcast(bf16[768,1536]{1,0:T(8,128)(2,1)} %param.7), dimensions={1,2} | broadcast | bytes 11796480 | tf_op jit(solution)/shard_map/stack | solution.py:11
  14.9 0.0 copy-start.4
  15.0 0.0 copy-start.1
  15.0 6.1 %all-to-all-start = ((bf16[4,768,1536]{2,1,0:T(8,128)(2,1)}), bf16[4,768,1536]{2,1,0:T(8,128)(2,1)}, u32[]{:S(2)}, u32[]{:S(2)}) async-start(bf16[4,768,1536]{2,1,0:T(8,128)(2,1)} %stack.2), calls=%async_computation | async-start | bytes 18874368 | tf_op jit(solution)/shard_map/all_to_all | solution.py:11
  21.1 0.0 copy-done.4
  21.1 0.3 dynamic-update-slice
  21.3 139.4 %all-reduce = f32[6144]{0:T(1024)S(1)} all-reduce(f32[6144]{0:T(1024)S(1)} %dynamic-update-slice), channel_id=1, replica_groups=mesh['bpm'=4,'cor'=8] {'bpm','cor'}, use_global_device_ids=true, to_apply=%add | all-reduce | flops 6144 | bytes 49152
  160.7 0.0 copy-done.1
  160.7 0.0 copy-start.2
  160.8 0.0 copy-start.3
  160.8 34.3 %gather_fusion = f32[6144]{0:T(1024)S(1)} fusion(f32[6144]{0:T(1024)S(1)} %all-reduce, s32[6144]{0:T(1024)S(1)} %get-tuple-element.5), kind=kCustom, calls=%fused_computation | custom fusion | bytes 73728 | tf_op jit(solution)/shard_map/gather | solution.py:9
  195.1 0.0 copy-done.2
  195.1 0.0 copy-done.3
  195.1 0.0 all-to-all-done
  195.1 12.7 %copy.11 = bf16[4,768,1536]{1,2,0:T(8,128)(2,1)} copy(bf16[4,768,1536]{2,1,0:T(8,128)(2,1)} %all-to-all-done) | data formatting | bytes 18874368 | tf_op jit(solution)/shard_map/all_to_all | solution.py:11
  207.8 0.0 all-gather.2.cloned.1.call-done
  207.8 0.0 copy-start
  207.8 11.6 %multiply_convert_fusion.2 = bf16[768,512]{1,0:T(8,128)(2,1)S(1)} fusion(bf16[6144,512]{0,1:T(8,128)(2,1)} %all-gather.2.cloned.1.call-done, bf16[768,6144]{0,1:T(8,128)(2,1)} %bitcast.10, f32[6144]{0:T(1024)S(1)} %gather_fusion, f32[512]{0:T(512)S(1)} %multiply_divide_fusion), kind=kOutput, calls=%fused_computation.7 | convolution fusion | flops 4846780416 | bytes 16541696 | tf_op jit(solution)/shard_map/dot_general | solution.py:16
  219.4 0.0 copy-done
  219.4 7.2 %fusion = f32[6144]{0:T(1024)S(1)} fusion(bf16[6144,512]{0,1:T(8,128)(2,1)} %all-gather.2.cloned.1.call-done, bf16[768,512]{1,0:T(8,128)(2,1)S(1)} %multiply_convert_fusion.2, bf16[768,6144]{0,1:T(8,128)(2,1)S(1)} %bitcast.11), kind=kOutput, calls=%fused_computation.4 | convolution fusion | flops 4841269248 | bytes 16539648 | tf_op jit(solution)/shard_map/dot_general | solution.py:18
  226.7 23.0 %scatter_custom_fusion = f32[6144]{0:T(1024)S(1)} fusion(s32[6144]{0:T(1024)S(1)} %get-tuple-element.6, f32[6144]{0:T(1024)S(1)} %fusion, f32[]{:T(128)} %constant.7.clone.1), kind=kCustom, calls=%fused_computation.10 | custom fusion | bytes 24580 | tf_op jit(solution)/shard_map/scatter | solution.py:22
  249.7 39.2 %psum.7 = f32[6144]{0:T(1024)S(1)} all-reduce(f32[6144]{0:T(1024)S(1)} %scatter_custom_fusion), channel_id=1, replica_groups=mesh['bpm'=4,'cor'=8] {'bpm','cor'}, use_global_device_ids=true, to_apply=%region_2.0 | all-reduce | flops 6144 | bytes 49152 | tf_op jit(solution)/shard_map/psum | solution.py:23
  288.9 0.6 dynamic_slice.3
  (3 shorter events, 0.0 us)
Async XLA Ops:
  6.5 201.3 %all-gather.2.cloned.1.call-start = ((), (), s32[]{:S(2)}) async-start(), calls=%async_computation.1 | async-start | bytes 7077888 | tf_op jit(solution)/shard_map/all_gather | solution.py:15
  14.9 6.1 %copy-start.4 = (f32[192]{0:T(256)S(1)}, f32[192]{0:T(256)}, u32[]{:S(2)}) copy-start(f32[192]{0:T(256)} %param.8) | copy-start | bytes 2308
  15.0 145.8 %copy-start.1 = (s32[6144]{0:T(1024)S(1)}, s32[6144]{0:T(1024)}, u32[]{:S(2)}) copy-start(s32[6144]{0:T(1024)} %param.9) | copy-start | bytes 73732
  15.0 180.1 %all-to-all-start = ((bf16[4,768,1536]{2,1,0:T(8,128)(2,1)}), bf16[4,768,1536]{2,1,0:T(8,128)(2,1)}, u32[]{:S(2)}, u32[]{:S(2)}) async-start(bf16[4,768,1536]{2,1,0:T(8,128)(2,1)} %stack.2), calls=%async_computation | async-start | bytes 18874368 | tf_op jit(solution)/shard_map/all_to_all | solution.py:11
  160.7 34.3 %copy-start.2 = (f32[512]{0:T(512)S(1)}, f32[512]{0:T(512)}, u32[]{:S(2)}) copy-start(f32[512]{0:T(512)} %param.11) | copy-start | bytes 6148
  160.8 34.3 %copy-start.3 = (s32[512]{0:T(512)S(1)}, s32[512]{0:T(512)}, u32[]{:S(2)}) copy-start(s32[512]{0:T(512)} %param.10) | copy-start | bytes 6148
  207.8 11.6 %copy-start = (bf16[4,768,1536]{1,2,0:T(8,128)(2,1)S(1)}, bf16[4,768,1536]{1,2,0:T(8,128)(2,1)}, u32[]{:S(2)}) copy-start(bf16[4,768,1536]{1,2,0:T(8,128)(2,1)} %copy.11) | copy-start | bytes 28311556
Sparse Core Ops, SparseCore 0:
  9.0 67.4 all-gather.1
